TPU v7x, 256 devices: a whole 4x4x8 slice. The times are simulated.
256 devices in a mesh: seq: 16 (over x, z_hi), mp: 16 (over y, z_lo, core).
Axes of the slice: x: 4, y: 4, z: 8 (z_hi: 4, z_lo: 2; z = z_hi * 2 + z_lo), core: 2. Of those that a mesh axis runs over, the one named last changes fastest.
Arguments:
- hidden: bfloat16 [4096, 4096], P('seq', 'mp'), may hold values from -6 to 6
- cotangent: bfloat16 [4096, 4096], P('seq', 'mp'), may hold values from -6 to 6
- neighbour_ids: int32 [64, 2, 128], P('seq'), may hold values from 0 to 63999
- neighbour_lengths: int32 [64, 2], replicated, may hold values from 1 to 128
- embed_table: bfloat16 [64000, 896], P('mp'), may hold values from -6 to 6
- enc_up: bfloat16 [3584, 896], P('mp'), may hold values from -0.1875 to 0.1875
- enc_down: bfloat16 [3584, 896], P('mp'), may hold values from -0.09375 to 0.09375
- w_query: bfloat16 [4096, 32, 128], P('seq', 'mp'), may hold values from -0.125 to 0.125
- w_keyval: bfloat16 [896, 32, 2, 128], P('seq', 'mp'), may hold values from -0.1875 to 0.1875
- w_out: bfloat16 [4096, 32, 128], P('seq', 'mp'), may hold values from -0.75 to 0.75
Outputs:
- cca_out: bfloat16 [4096, 4096], P('seq', 'mp')
- hidden_grad: bfloat16 [4096, 4096], P('seq', 'mp')
All inputs are finite; a program needn't handle non-finite values.
Results may differ from a plain program's by a relative error of at most 0.012.
Values may be sent and summed in bfloat16 or wider, within the bound.
A program may use at most 128 MiB of HBM per device.

v0:
```python
import jax
import jax.numpy as jnp
from jax import lax
from jax.sharding import PartitionSpec as P


def from_behind(shard, axis, by):
    count = lax.axis_size(axis)
    pairs = [(i, i + by) for i in range(count) if 0 <= i + by < count]
    return lax.ppermute(shard, axis, pairs)


def rms_rows(values):
    return values * lax.rsqrt(jnp.mean(values * values, axis=-1, keepdims=True) + 1e-06)


def shift_rows(flat, span_len):
    width = flat.shape[1]
    front = jnp.zeros((1, width), flat.dtype)
    back = jnp.zeros((span_len - 1, width), flat.dtype)
    return jnp.concatenate([front, flat, back], axis=0)


def contract_heads(left, right):
    return lax.dot_general(
        left, right, (((1,), (1,)), ((), ())), preferred_element_type=jnp.float32
    )


def per_device(
    hidden,
    cotangent,
    neighbour_ids,
    neighbour_lengths,
    embed_table,
    enc_up,
    enc_down,
    w_query,
    w_keyval,
    w_out,
):
    spans_here, neigh, nlen = neighbour_ids.shape
    tok_rows = hidden.shape[0]
    span_len = tok_rows // spans_here
    groups = spans_here + 1
    keys_per = neigh * nlen
    id_rows = spans_here * keys_per
    vocab_here = embed_table.shape[0]
    local_ids = neighbour_ids.reshape(id_rows) - lax.axis_index("mp") * vocab_here
    inside = jnp.logical_and(local_ids >= 0, local_ids < vocab_here)
    picked = jnp.take(embed_table, jnp.clip(local_ids, 0, vocab_here - 1), axis=0)
    masked = jnp.where(inside[:, None], picked, jnp.zeros((), picked.dtype))
    emb_share = (
        lax.psum_scatter(masked, "mp", scatter_dimension=0, tiled=True)
        .astype(jnp.float32)
        .astype(jnp.bfloat16)
    )
    emb = lax.all_gather(emb_share, "mp", axis=0, tiled=True)
    whole_hidden, whole_cot = (
        lax.all_gather(hidden, "mp", axis=1, tiled=True),
        lax.all_gather(cotangent, "mp", axis=1, tiled=True),
    )
    wq_full, wkv_full, wo_full = (
        lax.all_gather(w_query, "seq", axis=0, tiled=True),
        lax.all_gather(w_keyval, "seq", axis=0, tiled=True),
        lax.all_gather(w_out, "seq", axis=0, tiled=True),
    )
    width = whole_hidden.shape[1]
    heads_here = wq_full.shape[1]
    head_dim = wq_full.shape[2]
    inner = heads_here * head_dim
    scale = head_dim ** (-0.5)
    wq_flat = wq_full.reshape(width, inner)
    wo_flat = wo_full.reshape(width, inner)
    enc_width = emb.shape[1]
    wkv_flat = wkv_full.reshape(enc_width, 2 * inner)
    emb_wide = emb.astype(jnp.float32)
    normed = rms_rows(emb_wide).astype(jnp.bfloat16)
    act_cols = jax.nn.gelu(contract_heads(enc_up, normed)).astype(jnp.bfloat16)
    ffn_part = lax.dot_general(
        act_cols, enc_down, (((0,), (0,)), ((), ())), preferred_element_type=jnp.float32
    )
    total = lax.psum(ffn_part, "mp")
    encoded = rms_rows(emb_wide + total).astype(jnp.bfloat16)
    keyval = jnp.dot(encoded, wkv_flat, preferred_element_type=jnp.float32).astype(jnp.bfloat16)
    keyval = keyval.reshape(spans_here, keys_per, 2 * inner)
    last_rows = encoded.reshape(spans_here, keys_per, enc_width)[spans_here - 1]
    prev_rows = from_behind(last_rows, "seq", 1)
    previous = jnp.dot(prev_rows, wkv_flat, preferred_element_type=jnp.float32).astype(jnp.bfloat16)
    keyval_all = jnp.concatenate([previous[None], keyval], axis=0).reshape(
        groups, keys_per, heads_here, 2, head_dim
    )
    keys = keyval_all[:, :, :, 0]
    values = keyval_all[:, :, :, 1]
    position = lax.axis_index("seq")
    lens_pad = jnp.concatenate([jnp.ones((1, neigh), jnp.int32), neighbour_lengths], axis=0)
    lens = lax.dynamic_slice_in_dim(lens_pad, position * spans_here, groups, 0)
    key_mask = (jnp.arange(nlen, dtype=jnp.int32)[None, None, :] < lens[:, :, None]).reshape(
        groups, keys_per
    )
    valid = jnp.logical_or(jnp.arange(groups) > 0, position > 0).astype(jnp.float32)
    query = jnp.dot(whole_hidden, wq_flat, preferred_element_type=jnp.float32).astype(jnp.bfloat16)
    query_g = shift_rows(query, span_len).reshape(groups, span_len, heads_here, head_dim)
    scores = (
        jnp.einsum("gqhd,gkhd->ghqk", query_g, keys, preferred_element_type=jnp.float32) * scale
    )
    expo = jnp.where(key_mask[:, None, None, :], jnp.exp(scores), 0.0)
    prob = expo / jnp.sum(expo, axis=-1, keepdims=True) * valid[:, None, None, None]
    prob_low = prob.astype(jnp.bfloat16)
    attn = jnp.einsum(
        "ghqk,gkhd->gqhd", prob_low, values, preferred_element_type=jnp.float32
    ).astype(jnp.bfloat16)
    attn_flat = attn.reshape(groups * span_len, inner)[1 : tok_rows + 1]
    out_part = contract_heads(attn_flat, wo_flat)
    d_attn = jnp.dot(whole_cot, wo_flat, preferred_element_type=jnp.float32).astype(jnp.bfloat16)
    d_group = shift_rows(d_attn, span_len).reshape(groups, span_len, heads_here, head_dim)
    d_prob = jnp.einsum("gqhd,gkhd->ghqk", d_group, values, preferred_element_type=jnp.float32)
    delta = jnp.sum(prob * d_prob, axis=-1, keepdims=True)
    d_score = (prob * (d_prob - delta) * scale).astype(jnp.bfloat16)
    d_query = jnp.einsum(
        "ghqk,gkhd->gqhd", d_score, keys, preferred_element_type=jnp.float32
    ).astype(jnp.bfloat16)
    d_flat = d_query.reshape(groups * span_len, inner)[1 : tok_rows + 1]
    grad_part = contract_heads(d_flat, wq_flat)
    out_sum, grad_sum = (
        lax.psum_scatter(out_part, "mp", scatter_dimension=1, tiled=True),
        lax.psum_scatter(grad_part, "mp", scatter_dimension=1, tiled=True),
    )
    cca_out = out_sum.astype(jnp.bfloat16)
    hidden_grad = grad_sum.astype(jnp.bfloat16)
    return (cca_out, hidden_grad)


def solution(mesh):
    return jax.shard_map(
        per_device,
        mesh=mesh,
        in_specs=(
            P("seq", "mp"),
            P("seq", "mp"),
            P("seq", None, None),
            P(),
            P("mp", None),
            P("mp", None),
            P("mp", None),
            P("seq", "mp", None),
            P("seq", "mp", None, None),
            P("seq", "mp", None),
        ),
        out_specs=(P("seq", "mp"), P("seq", "mp")),
        check_vma=False,
    )
```

profile of v0, /device:TPU:4, one launch (start us, length us, event | category | flops | bytes accessed | tf_op | source)
XLA Modules:
  0.0 666.3 jit_solution(14386013505363016932)
XLA Ops:
  7.2 0.7 subtract_clamp_fusion
  8.0 0.7 compare_and_fusion
  8.7 8.6 %gather_fusion = bf16[1024,896]{1,0:T(8,128)(2,1)S(1)} fusion(bf16[4000,896]{1,0:T(8,128)(2,1)} %param.14, s32[1024]{0:T(1024)S(1)} %broadcast_clamp_fusion), kind=kCustom, calls=%fused_computation | custom fusion | bytes 3674112 | tf_op jit(solution)/shard_map/jit(_take)/gather | solution.py:51
  17.3 1.9 select_select_fusion
  19.3 69.7 %reduce-scatter.4.cloned.1.call-done = bf16[64,896]{1,0:T(8,128)(2,1)} async-done(((bf16[1024,896]{1,0:T(8,128)(2,1)}), bf16[64,896]{1,0:T(8,128)(2,1)}) %reduce-scatter.4.cloned.1.call-update) | async-done | bytes 114704 | tf_op jit(solution)/shard_map/reduce_scatter | solution.py:54
  89.1 0.7 all-gather.10.cloned.1.call-update
  89.8 0.5 all-gather.8.cloned.1.call-update
  90.4 0.5 all-gather.12.cloned.1.call-update
  91.0 0.5 all-gather.14.cloned.1.call-update
  91.5 33.0 %all-gather.6.cloned.1.call-done = bf16[1024,896]{1,0:T(8,128)(2,1)} async-done(((bf16[64,896]{1,0:T(8,128)(2,1)}), bf16[1024,896]{1,0:T(8,128)(2,1)}) %all-gather.6.cloned.1.call-update) | async-done | bytes 1835024 | tf_op jit(solution)/shard_map/all_gather | solution.py:58
  124.6 1.9 fusion.1
  126.5 4.9 fusion.50
  131.5 0.7 copy-done.9
  132.3 56.4 %all_gather.19 = bf16[896,2,2,128]{3,2,1,0:T(2,128)(2,1)S(1)} all-gather(bf16[56,2,2,128]{3,2,1,0:T(2,128)(2,1)S(1)} %copy-done.9), channel_id=1, replica_groups=mesh['seq'=16,'mp'=16] {'seq'}, dimensions={0}, use_global_device_ids=true | all-gather | bytes 974848 | tf_op jit(solution)/shard_map/all_gather | solution.py:65
  188.7 0.3 reshape.123
  189.4 3.3 all-gather.10.cloned.1.call-done
  192.7 38.4 %all-gather.8.cloned.1.call-done = bf16[256,4096]{1,0:T(8,128)(2,1)} async-done(((bf16[256,256]{1,0:T(8,128)(2,1)}), bf16[256,4096]{1,0:T(8,128)(2,1)}) %all-gather.8.cloned.1.call-update) | async-done | bytes 2097168 | tf_op jit(solution)/shard_map/all_gather | solution.py:60
  231.1 2.9 fusion.29
  234.0 58.4 %all-gather.12.cloned.1.call-done = bf16[4096,2,128]{2,1,0:T(2,128)(2,1)} async-done(((bf16[256,2,128]{2,1,0:T(2,128)(2,1)}), bf16[4096,2,128]{2,1,0:T(2,128)(2,1)}) %all-gather.12.cloned.1.call-update) | async-done | bytes 2097168 | tf_op jit(solution)/shard_map/all_gather | solution.py:66
  292.4 39.6 %all-gather.14.cloned.1.call-done = bf16[256,4096]{1,0:T(8,128)(2,1)} async-done(((bf16[256,256]{1,0:T(8,128)(2,1)}), bf16[256,4096]{1,0:T(8,128)(2,1)}) %all-gather.14.cloned.1.call-update) | async-done | bytes 2097168 | tf_op jit(solution)/shard_map/all_gather | solution.py:61
  332.0 3.1 fusion.32
  335.1 138.0 %all-reduce.3.cloned.1.call-done = f32[1024,896]{1,0:T(8,128)} async-done(((f32[1024,896]{1,0:T(8,128)}), f32[1024,896]{1,0:T(8,128)}) %all-reduce.3.cloned.1.call-update) | async-done | bytes 3670032 | tf_op jit(solution)/shard_map/psum | solution.py:83
  473.1 2.8 multiply_reduce_fusion
  475.9 0.3 copy-done.2
  476.3 0.5 multiply_convert_fusion
  476.8 1.3 copy-done.3
  478.0 0.8 slice.23
  478.8 4.4 collective-permute-start
  483.5 0.7 reshape.125
  484.2 0.7 reshape.128
  484.9 2.7 convolution_convert_fusion
  487.6 0.3 concatenate.18
  487.9 14.4 %collective-permute-done = bf16[256,896]{1,0:T(8,128)(2,1)} collective-permute-done((bf16[256,896]{1,0:T(8,128)(2,1)}, bf16[256,896]{1,0:T(8,128)(2,1)}, u32[]{:S(2)}, u32[]{:S(2)}) %collective-permute-start) | collective-permute-done | bytes 458784 | tf_op jit(solution)/shard_map/ppermute | solution.py:10
  502.3 1.4 convolution_convert_fusion.1
  503.9 0.3 copy_dynamic-update-slice_fusion
  504.3 0.3 fusion.54
  504.6 0.7 copy-done.7
  505.4 0.3 fusion.23
  505.7 0.8 copy-done.12
  506.5 1.1 divide_multiply_fusion
  507.6 1.9 fusion.36
  509.7 2.7 fusion.7
  512.5 2.0 fusion.35
  514.8 2.7 fusion.5
  517.5 66.1 %reduce-scatter.8.cloned.1.call-done = f32[256,256]{1,0:T(8,128)} async-done(((f32[256,4096]{1,0:T(8,128)}), f32[256,256]{1,0:T(8,128)}) %reduce-scatter.8.cloned.1.call-update) | async-done | bytes 262160 | tf_op jit(solution)/shard_map/reduce_scatter | solution.py:127
  583.7 1.6 convert_element_type.73
  585.3 72.8 %reduce-scatter.6.cloned.1.call-done = f32[256,256]{1,0:T(8,128)} async-done(((f32[256,4096]{1,0:T(8,128)}), f32[256,256]{1,0:T(8,128)}) %reduce-scatter.6.cloned.1.call-update) | async-done | bytes 262160 | tf_op jit(solution)/shard_map/reduce_scatter | solution.py:126
  658.1 1.6 convert_element_type.68
  (57 shorter events, 1.6 us)
Async XLA Ops:
  7.2 119.3 %copy-start = (bf16[224,896]{1,0:T(8,128)(2,1)S(1)}, bf16[224,896]{1,0:T(8,128)(2,1)}, u32[]{:S(2)}) copy-start(bf16[224,896]{1,0:T(8,128)(2,1)} %param.16) | copy-start | bytes 1204228
  7.2 81.8 %reduce-scatter.4.cloned.1.call-start = ((), (), s32[]{:S(2)}) async-start(), calls=%async_computation.3 | async-start | bytes 1949696 | tf_op jit(solution)/shard_map/reduce_scatter | solution.py:54
  19.2 107.3 %copy-start.11 = (bf16[224,896]{1,0:T(8,128)(2,1)S(1)}, bf16[224,896]{1,0:T(8,128)(2,1)}, u32[]{:S(2)}) copy-start(bf16[224,896]{1,0:T(8,128)(2,1)} %param.15) | copy-start | bytes 1204228
  19.2 105.4 %all-gather.6.cloned.1.call-start = ((), (), s32[]{:S(2)}) async-start(), calls=%async_computation.4 | async-start | bytes 1949696 | tf_op jit(solution)/shard_map/all_gather | solution.py:58
  89.0 103.6 %all-gather.10.cloned.1.call-start = ((), (), s32[]{:S(2)}) async-start(), calls=%async_computation.7 | async-start | bytes 2228224 | tf_op jit(solution)/shard_map/all_gather | solution.py:64
  89.7 141.3 %all-gather.8.cloned.1.call-start = ((), (), s32[]{:S(2)}) async-start(), calls=%async_computation.6 | async-start | bytes 2228224 | tf_op jit(solution)/shard_map/all_gather | solution.py:60
  90.3 202.1 %all-gather.12.cloned.1.call-start = ((), (), s32[]{:S(2)}) async-start(), calls=%async_computation.8 | async-start | bytes 2228224 | tf_op jit(solution)/shard_map/all_gather | solution.py:66
  90.9 241.1 %all-gather.14.cloned.1.call-start = ((), (), s32[]{:S(2)}) async-start(), calls=%async_computation.10 | async-start | bytes 2228224 | tf_op jit(solution)/shard_map/all_gather | solution.py:61
  91.5 381.7 %all-reduce.3.cloned.1.call-start = ((), (), s32[]{:S(2)}) async-start(), calls=%async_computation.5 | async-start | bytes 7340032 | tf_op jit(solution)/shard_map/psum | solution.py:83
  131.5 0.8 copy-start.9
  131.5 57.5 %copy-start.10 = (s32[64,2]{0,1:T(2,128)S(1)}, s32[64,2]{0,1:T(2,128)}, u32[]{:S(2)}) copy-start(s32[64,2]{0,1:T(2,128)} %param.13) | copy-start | bytes 1540
  131.5 452.2 %reduce-scatter.8.cloned.1.call-start = ((), (), s32[]{:S(2)}) async-start(), calls=%async_computation.11 | async-start | bytes 4456448 | tf_op jit(solution)/shard_map/reduce_scatter | solution.py:127
  332.0 141.1 %copy-start.1 = (bf16[1024,896]{1,0:T(8,128)(2,1)S(1)}, bf16[1024,896]{1,0:T(8,128)(2,1)}, u32[]{:S(2)}) copy-start(bf16[1024,896]{1,0:T(8,128)(2,1)} %all-gather.6.cloned.1.call-done) | copy-start | bytes 5505028
  473.1 3.1 copy-start.2
  476.8 1.3 copy-start.3
  478.8 23.5 %collective-permute-start = (bf16[256,896]{1,0:T(8,128)(2,1)}, bf16[256,896]{1,0:T(8,128)(2,1)}, u32[]{:S(2)}, u32[]{:S(2)}) collective-permute-start(bf16[256,896]{1,0:T(8,128)(2,1)} %slice.23), channel_id=1, source_target_pairs={{0,16},{16,32},{32,48},{48,64},{64,80},{80,96},{96,112},{112,128},... | collective-permute-start | bytes 1376264 | tf_op jit(solution)/shard_map/ppermute | solution.py:10
  487.9 16.3 %copy-start.6 = (bf16[5,64,2,128]{3,2,1,0:T(2,128)(2,1)S(1)}, bf16[5,64,2,128]{3,2,1,0:T(2,128)(2,1)}, u32[]{:S(2)}) copy-start(bf16[5,64,2,128]{3,2,1,0:T(2,128)(2,1)} %reshape.128) | copy-start | bytes 491524
  503.9 1.5 copy-start.8
  504.3 1.1 copy-start.7
  505.7 0.8 copy-start.12
  506.5 3.2 copy-start.5
  512.5 2.3 copy-start.4
  512.5 145.6 %reduce-scatter.6.cloned.1.call-start = ((), (), s32[]{:S(2)}) async-start(), calls=%async_computation.9 | async-start | bytes 4456448 | tf_op jit(solution)/shard_map/reduce_scatter | solution.py:126
Sparse Core Ops, SparseCore 0:
  19.3 69.6 reduce-scatter.3
  90.8 33.6 all-gather.5
  127.0 65.6 all-gather.9
  194.3 36.7 all-gather.7
  233.4 59.0 all-gather.11
  294.0 37.9 all-gather.13
  334.7 138.3 all-reduce.2
  512.6 71.0 reduce-scatter.7
  586.2 71.8 reduce-scatter.5
where the time goes:
time: 667 us; the launch traced here: 666 us
  waiting for transfers between devices  536 us (80%)
  blocking collectives  56.4 us (8%)
  matrix products  25.1 us (4%)
  local copies, waits for them, and re-layouts  16.6 us (2%)
  between operations  14.2 us (2%)
  other arithmetic  13 us (2%)
    psum x1, waiting for transfers between devices, per_device(): total = lax.psum(ffn_part, 'mp')  138 us
    reduce_scatter x1, waiting for transfers between devices, per_device(): lax.psum_scatter(out_part, 'mp', scatter_dimension=1, tiled=True)  72.8 us
    reduce_scatter x1, waiting for transfers between devices, per_device(): lax.psum_scatter(masked, 'mp', scatter_dimension=0, tiled=True)  69.7 us
    reduce_scatter x1, waiting for transfers between devices, per_device(): lax.psum_scatter(grad_part, 'mp', scatter_dimension=1, tiled=True)  66.1 us
    all_gather x1, waiting for transfers between devices, per_device(): lax.all_gather(w_out, 'seq', axis=0, tiled=True)  58.4 us
    all_gather x1, blocking collectives, per_device(): lax.all_gather(w_keyval, 'seq', axis=0, tiled=True)  56.4 us
    all_gather x1, waiting for transfers between devices, per_device(): lax.all_gather(cotangent, 'mp', axis=1, tiled=True)  39.6 us
    all_gather x1, waiting for transfers between devices, per_device(): lax.all_gather(hidden, 'mp', axis=1, tiled=True)  38.4 us
  transfers between devices with their start and end apart: 10, of which 10 were waited for; matrix products, arithmetic and copies ran while one was open for 4% of the time, Pallas kernels for 0%

commit v1 on v0

--- a/solution.py
+++ b/solution.py
@@ -58,7 +58,9 @@
     emb = lax.all_gather(emb_share, "mp", axis=0, tiled=True)
     whole_hidden, whole_cot = (
         lax.all_gather(hidden, "mp", axis=1, tiled=True),
-        lax.all_gather(cotangent, "mp", axis=1, tiled=True),
+        jnp.concatenate(
+            lax.all_to_all(jnp.stack([cotangent] * lax.axis_size("mp")), "mp", 0, 0), axis=1
+        ),
     )
     wq_full, wkv_full, wo_full = (
         lax.all_gather(w_query, "seq", axis=0, tiled=True),

time: 667 us -> 641 us (0.961)
  waiting for transfers between devices: 536 us -> 507 us
    all_gather x1 -> x0, waiting for transfers between devices: 39.6 us -> none  [per_device(): lax.all_gather(cotangent, 'mp', axis=1, tiled=True)]
    all_gather x1, waiting for transfers between devices: 33 us -> 43.1 us  [per_device(): emb = lax.all_gather(emb_share, 'mp', axis=0, tiled=True)]
  transfers between devices with their start and end apart: 10 -> 10, of which waited for: 10 -> 9; matrix products, arithmetic and copies ran while one was open for 4% -> 4% of each run, Pallas kernels for 0% -> 0%
where the time goes in v1:
time: 641 us; the launch traced here: 640 us
  waiting for transfers between devices  507 us (79%)
  blocking collectives  52.6 us (8%)
  matrix products  25.2 us (4%)
  local copies, waits for them, and re-layouts  18.2 us (3%)
  between operations  14.5 us (2%)
  other arithmetic  13 us (2%)
  starting transfers between devices  9.31 us (1%)
    psum x1, waiting for transfers between devices, per_device(): total = lax.psum(ffn_part, 'mp')  136 us
    reduce_scatter x1, waiting for transfers between devices, per_device(): lax.psum_scatter(out_part, 'mp', scatter_dimension=1, tiled=True)  72.4 us
    reduce_scatter x1, waiting for transfers between devices, per_device(): lax.psum_scatter(masked, 'mp', scatter_dimension=0, tiled=True)  69.7 us
    reduce_scatter x1, waiting for transfers between devices, per_device(): lax.psum_scatter(grad_part, 'mp', scatter_dimension=1, tiled=True)  66.2 us
    all_gather x1, waiting for transfers between devices, per_device(): lax.all_gather(w_out, 'seq', axis=0, tiled=True)  58.4 us
    all_gather x1, blocking collectives, per_device(): lax.all_gather(w_keyval, 'seq', axis=0, tiled=True)  52.6 us
    all_gather x1, waiting for transfers between devices, per_device(): emb = lax.all_gather(emb_share, 'mp', axis=0, tiled=True)  43.1 us
    all_gather x1, waiting for transfers between devices, per_device(): lax.all_gather(hidden, 'mp', axis=1, tiled=True)  39.4 us
  transfers between devices with their start and end apart: 10, of which 9 were waited for; matrix products, arithmetic and copies ran while one was open for 4% of the time, Pallas kernels for 0%

profile of v1, /device:TPU:4, one launch (start us, length us, event | category | flops | bytes accessed | tf_op | source)
XLA Modules:
  0.0 639.9 jit_solution(9649112858887469216)
XLA Ops:
  7.2 0.7 subtract_clamp_fusion
  8.0 0.7 compare_and_fusion
  8.7 8.6 %gather_fusion = bf16[1024,896]{1,0:T(8,128)(2,1)S(1)} fusion(bf16[4000,896]{1,0:T(8,128)(2,1)} %param.14, s32[1024]{0:T(1024)S(1)} %broadcast_clamp_fusion), kind=kCustom, calls=%fused_computation | custom fusion | bytes 3674112 | tf_op jit(solution)/shard_map/jit(_take)/gather | solution.py:51
  17.3 1.8 select_select_fusion
  19.3 69.7 %reduce-scatter.4.cloned.1.call-done = bf16[64,896]{1,0:T(8,128)(2,1)} async-done(((bf16[1024,896]{1,0:T(8,128)(2,1)}), bf16[64,896]{1,0:T(8,128)(2,1)}) %reduce-scatter.4.cloned.1.call-update) | async-done | bytes 114704 | tf_op jit(solution)/shard_map/reduce_scatter | solution.py:54
  89.1 0.7 all-gather.9.cloned.1.call-update
  89.8 0.5 all-gather.7.cloned.1.call-update
  90.4 0.5 all-gather.11.cloned.1.call-update
  91.0 1.5 stack.2
  92.5 4.6 all-to-all-start
  97.2 43.1 %all-gather.5.cloned.1.call-done = bf16[1024,896]{1,0:T(8,128)(2,1)} async-done(((bf16[64,896]{1,0:T(8,128)(2,1)}), bf16[1024,896]{1,0:T(8,128)(2,1)}) %all-gather.5.cloned.1.call-update) | async-done | bytes 1835024 | tf_op jit(solution)/shard_map/all_gather | solution.py:58
  140.3 1.9 fusion.1
  142.2 4.9 fusion.50
  147.2 0.7 copy-done.10
  148.0 52.6 %all_gather.16 = bf16[896,2,2,128]{3,2,1,0:T(2,128)(2,1)S(1)} all-gather(bf16[56,2,2,128]{3,2,1,0:T(2,128)(2,1)S(1)} %copy-done.10), channel_id=1, replica_groups=mesh['seq'=16,'mp'=16] {'seq'}, dimensions={0}, use_global_device_ids=true | all-gather | bytes 974848 | tf_op jit(solution)/shard_map/all_gather | solution.py:67
  200.6 0.3 reshape.131
  201.3 5.7 all-gather.9.cloned.1.call-done
  207.0 39.4 %all-gather.7.cloned.1.call-done = bf16[256,4096]{1,0:T(8,128)(2,1)} async-done(((bf16[256,256]{1,0:T(8,128)(2,1)}), bf16[256,4096]{1,0:T(8,128)(2,1)}) %all-gather.7.cloned.1.call-update) | async-done | bytes 2097168 | tf_op jit(solution)/shard_map/all_gather | solution.py:60
  246.4 2.9 fusion.29
  249.3 58.4 %all-gather.11.cloned.1.call-done = bf16[4096,2,128]{2,1,0:T(2,128)(2,1)} async-done(((bf16[256,2,128]{2,1,0:T(2,128)(2,1)}), bf16[4096,2,128]{2,1,0:T(2,128)(2,1)}) %all-gather.11.cloned.1.call-update) | async-done | bytes 2097168 | tf_op jit(solution)/shard_map/all_gather | solution.py:68
  307.7 3.1 fusion.32
  310.8 136.1 %all-reduce.3.cloned.1.call-done = f32[1024,896]{1,0:T(8,128)} async-done(((f32[1024,896]{1,0:T(8,128)}), f32[1024,896]{1,0:T(8,128)}) %all-reduce.3.cloned.1.call-update) | async-done | bytes 3670032 | tf_op jit(solution)/shard_map/psum | solution.py:85
  446.9 2.8 multiply_reduce_fusion
  449.7 0.3 copy-done.2
  450.1 0.5 multiply_convert_fusion
  450.5 1.3 copy-done.3
  451.8 0.8 slice.23
  452.6 4.4 collective-permute-start
  457.2 0.7 reshape.133
  457.9 0.7 reshape.138
  458.7 2.7 convolution_convert_fusion
  461.4 0.3 concatenate.18
  461.7 14.4 %collective-permute-done = bf16[256,896]{1,0:T(8,128)(2,1)} collective-permute-done((bf16[256,896]{1,0:T(8,128)(2,1)}, bf16[256,896]{1,0:T(8,128)(2,1)}, u32[]{:S(2)}, u32[]{:S(2)}) %collective-permute-start) | collective-permute-done | bytes 458784 | tf_op jit(solution)/shard_map/ppermute | solution.py:10
  476.1 1.4 convolution_convert_fusion.1
  477.7 0.3 copy_dynamic-update-slice_fusion
  478.0 0.4 fusion.54
  478.4 0.7 copy-done.7
  479.1 0.4 fusion.23
  479.5 0.8 copy-done.13
  480.3 1.1 divide_multiply_fusion
  481.4 1.9 fusion.36
  483.5 2.7 fusion.7
  486.3 2.0 fusion.35
  488.6 2.7 fusion.5
  491.3 66.2 %reduce-scatter.8.cloned.1.call-done = f32[256,256]{1,0:T(8,128)} async-done(((f32[256,4096]{1,0:T(8,128)}), f32[256,256]{1,0:T(8,128)}) %reduce-scatter.8.cloned.1.call-update) | async-done | bytes 262160 | tf_op jit(solution)/shard_map/reduce_scatter | solution.py:129
  557.5 1.6 convert_element_type.73
  559.1 72.4 %reduce-scatter.6.cloned.1.call-done = f32[256,256]{1,0:T(8,128)} async-done(((f32[256,4096]{1,0:T(8,128)}), f32[256,256]{1,0:T(8,128)}) %reduce-scatter.6.cloned.1.call-update) | async-done | bytes 262160 | tf_op jit(solution)/shard_map/reduce_scatter | solution.py:128
  631.5 1.6 convert_element_type.68
  (60 shorter events, 1.6 us)
Async XLA Ops:
  7.2 135.0 %copy-start = (bf16[224,896]{1,0:T(8,128)(2,1)S(1)}, bf16[224,896]{1,0:T(8,128)(2,1)}, u32[]{:S(2)}) copy-start(bf16[224,896]{1,0:T(8,128)(2,1)} %param.16) | copy-start | bytes 1204228
  7.2 81.8 %reduce-scatter.4.cloned.1.call-start = ((), (), s32[]{:S(2)}) async-start(), calls=%async_computation.4 | async-start | bytes 1949696 | tf_op jit(solution)/shard_map/reduce_scatter | solution.py:54
  17.3 73.6 %copy-start.9 = (bf16[256,256]{1,0:T(8,128)(2,1)S(1)}, bf16[256,256]{1,0:T(8,128)(2,1)}, u32[]{:S(2)}) copy-start(bf16[256,256]{1,0:T(8,128)(2,1)} %param.11) | copy-start | bytes 393220
  19.2 121.0 %all-gather.5.cloned.1.call-start = ((), (), s32[]{:S(2)}) async-start(), calls=%async_computation.5 | async-start | bytes 1949696 | tf_op jit(solution)/shard_map/all_gather | solution.py:58
  89.0 117.9 %all-gather.9.cloned.1.call-start = ((), (), s32[]{:S(2)}) async-start(), calls=%async_computation.8 | async-start | bytes 2228224 | tf_op jit(solution)/shard_map/all_gather | solution.py:66
  89.8 156.6 %all-gather.7.cloned.1.call-start = ((), (), s32[]{:S(2)}) async-start(), calls=%async_computation.7 | async-start | bytes 2228224 | tf_op jit(solution)/shard_map/all_gather | solution.py:60
  90.3 217.4 %all-gather.11.cloned.1.call-start = ((), (), s32[]{:S(2)}) async-start(), calls=%async_computation.9 | async-start | bytes 2228224 | tf_op jit(solution)/shard_map/all_gather | solution.py:68
  92.5 49.7 %copy-start.12 = (bf16[224,896]{1,0:T(8,128)(2,1)S(1)}, bf16[224,896]{1,0:T(8,128)(2,1)}, u32[]{:S(2)}) copy-start(bf16[224,896]{1,0:T(8,128)(2,1)} %param.15) | copy-start | bytes 1204228
  92.5 215.2 %all-to-all-start = ((bf16[16,256,256]{1,2,0:T(8,128)(2,1)}), bf16[16,256,256]{1,2,0:T(8,128)(2,1)}, u32[]{:S(2)}, u32[]{:S(2)}) async-start(bf16[16,256,256]{1,2,0:T(8,128)(2,1)} %stack.2), calls=%async_computation.2 | async-start | bytes 4194304 | tf_op jit(solution)/shard_map/all_to_all | solution.py:62
  97.1 349.8 %all-reduce.3.cloned.1.call-start = ((), (), s32[]{:S(2)}) async-start(), calls=%async_computation.6 | async-start | bytes 7340032 | tf_op jit(solution)/shard_map/psum | solution.py:85
  147.1 0.8 copy-start.10
  147.2 53.8 %copy-start.11 = (s32[64,2]{0,1:T(2,128)S(1)}, s32[64,2]{0,1:T(2,128)}, u32[]{:S(2)}) copy-start(s32[64,2]{0,1:T(2,128)} %param.13) | copy-start | bytes 1540
  147.2 410.3 %reduce-scatter.8.cloned.1.call-start = ((), (), s32[]{:S(2)}) async-start(), calls=%async_computation.11 | async-start | bytes 4456448 | tf_op jit(solution)/shard_map/reduce_scatter | solution.py:129
  307.7 139.2 %copy-start.1 = (bf16[1024,896]{1,0:T(8,128)(2,1)S(1)}, bf16[1024,896]{1,0:T(8,128)(2,1)}, u32[]{:S(2)}) copy-start(bf16[1024,896]{1,0:T(8,128)(2,1)} %all-gather.5.cloned.1.call-done) | copy-start | bytes 5505028
  446.9 3.1 copy-start.2
  450.5 1.3 copy-start.3
  452.6 23.5 %collective-permute-start = (bf16[256,896]{1,0:T(8,128)(2,1)}, bf16[256,896]{1,0:T(8,128)(2,1)}, u32[]{:S(2)}, u32[]{:S(2)}) collective-permute-start(bf16[256,896]{1,0:T(8,128)(2,1)} %slice.23), channel_id=1, source_target_pairs={{0,16},{16,32},{32,48},{48,64},{64,80},{80,96},{96,112},{112,128},... | collective-permute-start | bytes 1376264 | tf_op jit(solution)/shard_map/ppermute | solution.py:10
  461.7 16.3 %copy-start.6 = (bf16[5,64,2,128]{3,2,1,0:T(2,128)(2,1)S(1)}, bf16[5,64,2,128]{3,2,1,0:T(2,128)(2,1)}, u32[]{:S(2)}) copy-start(bf16[5,64,2,128]{3,2,1,0:T(2,128)(2,1)} %reshape.138) | copy-start | bytes 491524
  477.6 1.5 copy-start.8
  478.0 1.1 copy-start.7
  479.5 0.8 copy-start.13
  480.3 3.2 copy-start.5
  486.3 2.3 copy-start.4
  486.3 145.2 %reduce-scatter.6.cloned.1.call-start = ((), (), s32[]{:S(2)}) async-start(), calls=%async_computation.10 | async-start | bytes 4456448 | tf_op jit(solution)/shard_map/reduce_scatter | solution.py:128
Sparse Core Ops, SparseCore 0:
  19.3 69.6 reduce-scatter.3
  90.8 49.3 all-gather.4
  142.7 64.2 all-gather.8
  208.6 37.7 all-gather.6
  248.6 59.0 all-gather.10
  310.2 136.6 all-reduce.2
  486.4 71.0 reduce-scatter.7
  560.0 71.4 reduce-scatter.5
